TPU v7x, 32 devices: a whole 2x2x4 slice. The times are simulated.
32 devices in a mesh: tenant: 2 (over x), row: 16 (over z, y, core).
Axes of the slice: x: 2, y: 2, z: 4, core: 2. Of those that a mesh axis runs over, the one named last changes fastest.
Arguments:
- queries: bfloat16 [4096, 256], P(('tenant', 'row')), parts along dimension 0, may hold values from -6 to 6
- probes: int32 [4096, 16], P(('tenant', 'row')), parts along dimension 0, may hold values from 0 to 143, all different within a row; in each aligned block of 128 rows (0 to 127, 128 to 255, ...) at most 32 rows name the same one
- hot_lists: bfloat16 [32, 256, 256], P('tenant'), parts along dimension 0, may hold values from -0.375 to 0.375
- cold_lists: bfloat16 [256, 256, 256], P(('tenant', 'row')), parts along dimension 0, may hold values from -0.375 to 0.375
Outputs:
- nearest: float32 [4096, 128], P(('tenant', 'row')), parts along dimension 0
There are 2 independent parts, one for each index of `tenant`. A program takes and returns all parts, laid end to end along the dimension named above; each array names one. Nothing has to cross between parts.
Inputs may be any that keep to these rules, and one draw needn't show every extreme that they name: `probes`: each query names 16 different lists; every list is named by some query. Within the queries of one index of row (aligned blocks of 128 rows) no list is named more than 32 times, a bound that some block reaches.
All inputs are finite; a program needn't handle non-finite values.
Results may differ from a plain program's by a relative error of at most 0.0003.
Values may be sent and summed in bfloat16 or wider, within the bound.
A program may use at most 64 MiB of HBM per device.

v0:
```python
import math

import jax
import jax.numpy as jnp
from jax import lax
from jax.sharding import PartitionSpec as P

TOPK = 128


def hot_scores(queries, hot_lists):
    hot_count, lsize, width = hot_lists.shape
    qcount = queries.shape[0]
    flat_hot = hot_lists.reshape(hot_count * lsize, width)
    scores = lax.dot_general(
        queries, flat_hot, (((1,), (1,)), ((), ())), preferred_element_type=jnp.float32
    )
    return scores.reshape(qcount, hot_count, lsize)


def earlier_equal(flat):
    count = flat.shape[0]
    block = math.gcd(count, 512)
    index_all = jnp.arange(count, dtype=jnp.int32)

    def one_block(start):
        ids = lax.dynamic_slice_in_dim(flat, start, block, 0)
        where_at = start + jnp.arange(block, dtype=jnp.int32)
        same = (ids[:, None] == flat[None, :]) & (index_all[None, :] < where_at[:, None])
        return jnp.sum(same.astype(jnp.int32), axis=1)

    starts = jnp.arange(count // block, dtype=jnp.int32) * block
    return lax.map(one_block, starts).reshape(count)


def shards(queries, probes, hot_lists, cold_lists):
    rows = lax.axis_size("row")
    qcount, nprobe = probes.shape
    list_dev = cold_lists.shape[0]
    hot_count, lsize, width = hot_lists.shape
    capacity = 2 * ((qcount * nprobe + list_dev * rows - 1) // (list_dev * rows))
    total = rows * list_dev * capacity
    flat = probes.reshape(-1)
    count = flat.shape[0]
    pair_query = jnp.arange(count, dtype=jnp.int32) // nprobe
    rank = earlier_equal(flat)
    cold_id = flat - hot_count
    is_cold = cold_id >= 0
    slot = jnp.where(is_cold, cold_id * capacity + rank, total)
    outgoing = (
        jnp.zeros((total, width), jnp.bfloat16).at[slot].set(queries[pair_query], mode="drop")
    )
    outgoing = outgoing.reshape(rows, list_dev, capacity, width)
    arrived = lax.all_to_all(outgoing, "row", split_axis=0, concat_axis=0, tiled=True)
    scores = jnp.einsum("slcd,lvd->slcv", arrived, cold_lists, preferred_element_type=jnp.float32)
    reading = jnp.minimum(slot, total - 1)
    returned = lax.all_to_all(scores, "row", split_axis=0, concat_axis=0, tiled=True).reshape(
        total, lsize
    )
    cold_rows = returned[reading]
    hot_all = hot_scores(queries, hot_lists)
    hot_pick = jnp.clip(probes, 0, hot_count - 1)
    hot_rows = jnp.take_along_axis(hot_all, hot_pick[:, :, None], axis=1).reshape(count, lsize)
    merged = jnp.where(is_cold[:, None], cold_rows, hot_rows).reshape(qcount, nprobe * lsize)
    return lax.top_k(merged, TOPK)[0]


def solution(mesh):
    placed = (
        P(("tenant", "row"), None),
        P(("tenant", "row"), None),
        P("tenant", None, None),
        P(("tenant", "row"), None, None),
    )
    return jax.shard_map(
        shards, mesh=mesh, in_specs=placed, out_specs=P(("tenant", "row"), None), check_vma=False
    )
```

profile of v0, /device:TPU:13, one launch (start us, length us, event | category | flops | bytes accessed | tf_op | source)
XLA Modules:
  0.0 350.8 jit_solution(5414763663897539160)
XLA Ops:
  0.0 0.9 copy.31
  1.1 0.7 compare_and_fusion
  1.8 0.7 add_multiply_fusion
  2.6 18.6 %while.12 = (s32[]{:T(128)}, s32[4,512]{1,0:T(4,128)S(1)}, s32[4]{0:T(128)S(1)}, s32[2048]{0:T(1024)S(1)}, s32[128,16]{1,0:T(8,128)}, /*index=5*/s32[2048]{0:T(1024)S(1)}, s32[]{:T(128)}, s32[]{:T(128)}, s32[]{:T(128)}) while((s32[]{:T(128)}, s32[4,512]{1,0:T(4,128)S(1)}, s32[4]{0:T(128)S(1)}, s32[2048]{0:T(1024)S(1)}, ...), condition=%wide.wide.region_2.3_spmd.clone, body=%wide.wide.region_0.2_spmd.clone.sunk | while | flops 5242885 | bytes 24727 | solution.py:33
  5.4 0.7 iota_add_fusion.3
  6.1 1.1 convert_reduce_fusion.3
  7.2 0.7 dynamic_slice.13
  10.0 0.7 iota_add_fusion.3
  10.7 1.1 convert_reduce_fusion.3
  14.7 0.7 iota_add_fusion.3
  15.4 1.1 convert_reduce_fusion.3
  19.3 0.7 iota_add_fusion.3
  20.0 1.1 convert_reduce_fusion.3
  21.6 26.7 %scatter_custom_fusion = bf16[4096,256]{1,0:T(8,128)(2,1)} fusion(s32[2048]{0:T(1024)S(1)} %bitcast.47, bf16[128,256]{1,0:T(8,128)(2,1)} %param.6, s32[2048]{0:T(1024)S(1)} %broadcast_clamp_fusion.1, bf16[]{:T(256)} %constant.55.clone.1), kind=kCustom, calls=%fused_computation.12 | custom fusion | bytes 2097664 | tf_op jit(solution)/shard_map/scatter | solution.py:51
  48.4 53.9 %all_to_all.10 = bf16[16,8,32,256]{3,2,1,0:T(8,128)(2,1)S(1)} all-to-all(bf16[16,8,32,256]{3,2,1,0:T(8,128)(2,1)} %bitcast.39), channel_id=1, replica_groups=mesh['tenant'=2,'row'=16] {'row'}, dimensions={0} | all-to-all | bytes 4194304 | tf_op jit(solution)/shard_map/all_to_all | solution.py:54
  102.3 0.7 convolution_bitcast_fusion
  103.0 2.3 copy.34
  105.3 5.2 %all-to-all-start.1 = ((f32[16,8,32,256]{3,2,1,0:T(8,128)}), f32[16,8,32,256]{3,2,1,0:T(8,128)}, u32[]{:S(2)}, u32[]{:S(2)}) async-start(f32[16,8,32,256]{3,2,1,0:T(8,128)} %copy.34), calls=%async_computation.1 | async-start | bytes 8388608 | tf_op jit(solution)/shard_map/all_to_all | solution.py:57
  111.4 0.8 fusion.8
  112.2 2.6 copy.37
  115.0 39.7 %gather_fusion.1 = f32[2048,256]{1,0:T(8,128)} fusion(f32[128,16,256]{2,1,0:T(8,128)} %copy.37, s32[2048]{0:T(1024)S(1)} %reshape.175), kind=kCustom, calls=%fused_computation.2 | custom fusion | bytes 4210688 | tf_op jit(solution)/shard_map/jit(take_along_axis)/gather | solution.py:63
  154.7 1.9 broadcast_select_fusion
  156.6 3.0 copy.45
  159.7 43.3 %all-to-all-done.1 = f32[16,8,32,256]{3,2,1,0:T(8,128)} async-done(((f32[16,8,32,256]{3,2,1,0:T(8,128)}), f32[16,8,32,256]{3,2,1,0:T(8,128)}, u32[]{:S(2)}, u32[]{:S(2)}) %all-to-all-start.1) | async-done | bytes 4194336 | tf_op jit(solution)/shard_map/all_to_all | solution.py:57
  203.0 10.8 %gather_fusion = f32[2048,256]{1,0:T(8,128)} fusion(f32[4096,256]{1,0:T(8,128)} %bitcast.6, s32[2048]{0:T(1024)S(1)} %broadcast_clamp_fusion), kind=kCustom, calls=%fused_computation.1 | custom fusion | bytes 4202496 | tf_op jit(solution)/shard_map/gather | solution.py:60
  213.7 2.7 gather.14
  216.4 3.9 %select_n.90 = f32[128,4096]{1,0:T(8,128)} select(pred[128,4096]{1,0:T(8,128)(4,1)S(1)} %bitcast.42, f32[128,4096]{1,0:T(8,128)} %gather.14, f32[128,4096]{1,0:T(8,128)} %bitcast.38) | non-fusion elementwise | flops 524288 | bytes 6815744 | tf_op jit(solution)/shard_map/jit(_where)/select_n | solution.py:64
  220.3 2.9 copy.39
  223.2 1.4 iota.21.clone
  224.7 121.8 %top_k.9 = (f32[128,4096]{0,1:T(8,128)}, s32[128,4096]{0,1:T(8,128)}) sort(f32[128,4096]{0,1:T(8,128)} %copy.39, s32[128,4096]{0,1:T(8,128)} %iota.21.clone), dimensions={1}, to_apply=%region_4.5 | sort | flops 9961472 | bytes 8388608 | tf_op jit(solution)/shard_map/top_k | solution.py:65
  346.4 2.9 copy.41
  349.3 1.5 top_k.11
  (40 shorter events, 4.2 us)
Async XLA Ops:
  0.0 111.4 %copy-start = (bf16[16,256,256]{2,1,0:T(8,128)(2,1)S(1)}, bf16[16,256,256]{2,1,0:T(8,128)(2,1)}, u32[]{:S(2)}) copy-start(bf16[16,256,256]{2,1,0:T(8,128)(2,1)} %param.8) | copy-start | bytes 6291460
  0.9 1.6 copy-start.2
  48.4 53.9 %copy-start.1 = (bf16[8,256,256]{2,1,0:T(8,128)(2,1)S(1)}, bf16[8,256,256]{2,1,0:T(8,128)(2,1)}, u32[]{:S(2)}) copy-start(bf16[8,256,256]{2,1,0:T(8,128)(2,1)} %param.9) | copy-start | bytes 3145732
  105.3 6.0 %copy-start.4 = (bf16[128,256]{1,0:T(8,128)(2,1)S(1)}, bf16[128,256]{1,0:T(8,128)(2,1)}, u32[]{:S(2)}) copy-start(bf16[128,256]{1,0:T(8,128)(2,1)} %param.6) | copy-start | bytes 196612
  105.3 97.6 %all-to-all-start.1 = ((f32[16,8,32,256]{3,2,1,0:T(8,128)}), f32[16,8,32,256]{3,2,1,0:T(8,128)}, u32[]{:S(2)}, u32[]{:S(2)}) async-start(f32[16,8,32,256]{3,2,1,0:T(8,128)} %copy.34), calls=%async_computation.1 | async-start | bytes 8388608 | tf_op jit(solution)/shard_map/all_to_all | solution.py:57
  112.2 2.6 copy-start.3
where the time goes:
time: 353 us; the launch traced here: 351 us
  other arithmetic  136 us (39%)
  local copies, waits for them, and re-layouts  102 us (29%)
  blocking collectives  53.9 us (15%)
  waiting for transfers between devices  43.3 us (12%)
  loops' own time  8.4 us (2%)
  starting transfers between devices  5.15 us (1%)
    top_k x1, other arithmetic, shards(): return lax.top_k(merged, TOPK)[0]  122 us
    all_to_all x1, blocking collectives, shards(): lax.all_to_all(outgoing, 'row', split_axis=0, concat_axis=0, tiled=True)  53.9 us
    all_to_all x1, waiting for transfers between devices, shards(): lax.all_to_all(scores, 'row', split_axis=0, concat_axis=0, tiled=True)  43.3 us
    gather x3, local copies, waits for them, and re-layouts, shards(): jnp.take_along_axis(hot_all, hot_pick[:, :, None], axis=1)  39.9 us
    scatter x1, local copies, waits for them, and re-layouts, shards(): jnp.zeros((total, width), jnp.bfloat16).at[slot]  26.7 us
    gather x2, local copies, waits for them, and re-layouts, shards(): cold_rows = returned[reading]  13.5 us
    another operation x1, loops' own time, earlier_equal(): return lax.map(one_block, starts).reshape(count)  8.4 us
    unnamed x15, local copies, waits for them, and re-layouts  7.22 us
  transfers between devices with their start and end apart: 1, of which 1 were waited for; matrix products, arithmetic and copies ran while one was open for 14% of the time, Pallas kernels for 0%

commit v1 on v0

--- a/solution.py
+++ b/solution.py
@@ -1,11 +1,17 @@
+import functools
 import math
 
 import jax
 import jax.numpy as jnp
 from jax import lax
+from jax.experimental import pallas as pl
+from jax.experimental.pallas import tpu as pltpu
 from jax.sharding import PartitionSpec as P
 
 TOPK = 128
+LOW = -3.0e38
+SUB = 8
+LANES = 128
 
 
 def hot_scores(queries, hot_lists):
@@ -33,7 +39,7 @@
     return lax.map(one_block, starts).reshape(count)
 
 
-def shards(queries, probes, hot_lists, cold_lists):
+def general(queries, probes, hot_lists, cold_lists):
     rows = lax.axis_size("row")
     qcount, nprobe = probes.shape
     list_dev = cold_lists.shape[0]
@@ -65,6 +71,350 @@
     return lax.top_k(merged, TOPK)[0]
 
 
+def batcher(n):
+    pairs = []
+    p = 1
+    while p < n:
+        k = p
+        while k >= 1:
+            for j in range(k % p, n - k, 2 * k):
+                for i in range(min(k, n - j - k)):
+                    if (i + j) // (2 * p) == (i + j + k) // (2 * p):
+                        pairs.append((i + j, i + j + k))
+            k //= 2
+        p *= 2
+    return pairs
+
+
+def exchange(vals, a, b):
+    x, y = vals[a], vals[b]
+    vals[a], vals[b] = jnp.maximum(x, y), jnp.minimum(x, y)
+
+
+def clean(vals, where, dists):
+    for d in dists:
+        for i in range(len(where)):
+            if i & d == 0:
+                exchange(vals, where[i], where[i + d])
+
+
+def at(i):
+    return pl.ds(pl.multiple_of(i * SUB, SUB), SUB)
+
+
+def loop(n, unroll, body):
+    @pl.loop(0, n // unroll)
+    def _(step):
+        for u in range(unroll):
+            body(step * unroll + u)
+
+
+def sort_runs(ref, count):
+    net = batcher(32)
+
+    def body(t):
+        vals = [ref[at(t * 32 + i), :] for i in range(32)]
+        for a, b in net:
+            exchange(vals, a, b)
+        for i in range(32):
+            ref[at(t * 32 + i), :] = vals[i]
+
+    loop(count // 32, 1, body)
+
+
+def join_runs(ref, count, half):
+    size = 2 * half
+    step = half // 4
+    per = 4
+
+    @pl.loop(0, count // size * step // per)
+    def _(t):
+        base = t * per // step * size
+        first = t * per % step
+        work = []
+        for u in range(per):
+            i = first + u
+            idx = [base + i + step * k for k in range(4)]
+            idx += [base + size - 1 - i - step * k for k in range(4)]
+            work.append((idx, [ref[at(x), :] for x in idx]))
+        for _, vals in work:
+            for k in range(4):
+                exchange(vals, k, 4 + k)
+            clean(vals, [0, 1, 2, 3], (2, 1))
+            clean(vals, [7, 6, 5, 4], (2, 1))
+        for idx, vals in work:
+            for x, v in zip(idx, vals):
+                ref[at(x), :] = v
+
+    tidy(ref, ref, count, step)
+
+
+def tidy(src, dst, count, block):
+    dists = []
+    d = block // 2
+    while d:
+        dists.append(d)
+        d //= 2
+
+    @pl.loop(0, count // 32)
+    def _(t):
+        vals = [src[at(t * 32 + i), :] for i in range(32)]
+        for c in range(32 // block):
+            clean(vals, list(range(c * block, (c + 1) * block)), dists)
+        for i in range(32):
+            dst[at(t * 32 + i), :] = vals[i]
+
+
+def best_of(a, abase, b, bbase, tmp, dst, turn=0):
+    step = TOPK // 8
+    per = 2
+
+    @pl.loop(0, step // per)
+    def _(t):
+        work = []
+        for u in range(per):
+            i = t * per + u
+            vals = []
+            for k in range(8):
+                x = a[at(abase + i + step * k), :]
+                y = b[at(bbase + TOPK - 1 - i - step * k), :]
+                if turn:
+                    y = pltpu.roll(y, turn, 0)
+                vals.append(jnp.maximum(x, y))
+            work.append(vals)
+        for vals in work:
+            clean(vals, list(range(8)), (4, 2, 1))
+        for u, vals in enumerate(work):
+            for k in range(8):
+                tmp[at(t * per + u + step * k), :] = vals[k]
+
+    tidy(tmp, dst, TOPK, step)
+
+
+def fused(
+    rows, cap, q_ref, pt_ref, hot_ref, cold_ref, out_ref,
+    q_all, pt_all, key, onehot, work, short, tmp, runs, hotbest, sendbuf, recv,
+    qs_sem, qr_sem, ps_sem, pr_sem, ss_sem, sr_sem,
+):
+    me = lax.axis_index("row")
+    qcount = q_ref.shape[0]
+    hot_count, lsize = hot_ref.shape[0], hot_ref.shape[1]
+    list_dev = cold_ref.shape[0]
+    nprobe = pt_ref.shape[0]
+    pack = LANES // cap
+    f32 = jnp.float32
+
+    def peer(b):
+        return {"row": b}
+
+    def q_copy(b, slot):
+        return pltpu.make_async_remote_copy(
+            src_ref=q_ref, dst_ref=q_all.at[slot], send_sem=qs_sem.at[b], recv_sem=qr_sem.at[slot],
+            device_id=peer(b), device_id_type=pl.DeviceIdType.MESH,
+        )
+
+    def p_copy(b, slot):
+        return pltpu.make_async_remote_copy(
+            src_ref=pt_ref, dst_ref=pt_all.at[slot], send_sem=ps_sem.at[b], recv_sem=pr_sem.at[slot],
+            device_id=peer(b), device_id_type=pl.DeviceIdType.MESH,
+        )
+
+    def s_copy(b, slot):
+        return pltpu.make_async_remote_copy(
+            src_ref=sendbuf.at[b], dst_ref=recv.at[slot], send_sem=ss_sem.at[b],
+            recv_sem=sr_sem.at[slot], device_id=peer(b), device_id_type=pl.DeviceIdType.MESH,
+        )
+
+    barrier = pltpu.get_barrier_semaphore()
+
+    @pl.loop(1, rows)
+    def _(d):
+        pl.semaphore_signal(
+            barrier, inc=1, device_id=peer(lax.rem(me + d, rows)), device_id_type=pl.DeviceIdType.MESH
+        )
+
+    pl.semaphore_wait(barrier, rows - 1)
+
+    @pl.loop(1, rows)
+    def _(d):
+        b = lax.rem(me + d, rows)
+        p_copy(b, me).start()
+        q_copy(b, me).start()
+
+    q_all[me] = q_ref[...]
+    pt_all[me] = pt_ref[...]
+
+    before = (
+        lax.broadcasted_iota(jnp.int32, (qcount, qcount), 0)
+        < lax.broadcasted_iota(jnp.int32, (qcount, qcount), 1)
+    )
+    before = jnp.where(before, 1.0, 0.0).astype(jnp.bfloat16)
+
+    def keys_of(pt, first, count):
+        ids = first + lax.broadcasted_iota(jnp.int32, (count, qcount), 0)
+        named = pt[0:1, :] == ids
+        for j in range(1, nprobe):
+            named = named | (pt[j : j + 1, :] == ids)
+        ones = jnp.where(named, 1.0, 0.0)
+        rank = jnp.dot(ones.astype(jnp.bfloat16), before, preferred_element_type=f32)
+        return named, rank
+
+    slot_row = lax.broadcasted_iota(jnp.int32, (LANES, pack * qcount), 0).astype(f32)
+    lane = lax.broadcasted_iota(jnp.int32, (lsize, LANES), 1)
+
+    def match(l):
+        hit = slot_row == key[l : l + 1, :]
+        hot1 = jnp.where(hit, 1.0, 0.0).astype(jnp.bfloat16)
+        onehot[l] = hot1
+        return hot1
+
+    def spread(l, half):
+        part = short[pl.ds(l, TOPK, stride=SUB), :]
+        high = part.astype(jnp.bfloat16)
+        low = (part - high.astype(f32)).astype(jnp.bfloat16)
+        hot1 = onehot[l]
+        full = jnp.dot(high, hot1, preferred_element_type=f32)
+        full = full + jnp.dot(low, hot1, preferred_element_type=f32)
+        full = jnp.where(key[l : l + 1, :] >= 0.0, full, LOW)
+        for b in range(pack):
+            runs[l // half, pl.ds((l % half) * pack + b, TOPK, stride=SUB), :] = full[
+                :, b * qcount : (b + 1) * qcount
+            ]
+
+    def shorten():
+        sort_runs(work, lsize)
+        join_runs(work, lsize, 32)
+        join_runs(work, lsize, 64)
+        best_of(work, 0, work, TOPK, tmp, short)
+
+    half = SUB // pack
+
+    named, rank = keys_of(pt_ref[...], 0, hot_count)
+    for l in range(hot_count):
+        value = jnp.where(named[l : l + 1, :], rank[l : l + 1, :] + float(cap * (l % pack)), -1.0)
+        key[l // pack : l // pack + 1, (l % pack) * qcount : (l % pack + 1) * qcount] = value
+    mine = q_ref[...]
+    stack = jnp.concatenate([mine] * pack, axis=0)
+    for t in range(hot_count // pack):
+        rows_t = jnp.dot(match(t), stack, preferred_element_type=f32).astype(jnp.bfloat16)
+        score = None
+        for c in range(pack):
+            one = lax.dot_general(
+                hot_ref[t * pack + c], rows_t, (((1,), (1,)), ((), ())), preferred_element_type=f32
+            )
+            score = one if score is None else jnp.where(lane >= c * cap, one, score)
+        work[pl.ds(t, lsize, stride=SUB), :] = score
+        if hot_count // pack + t < SUB:
+            work[pl.ds(hot_count // pack + t, lsize, stride=SUB), :] = score
+    shorten()
+    for t in range(hot_count // pack):
+        spread(t, half)
+    best_of(runs.at[0], 0, runs.at[1], 0, tmp, hotbest)
+
+    groups = rows // pack
+
+    @pl.loop(0, groups)
+    def _(step):
+        g = lax.rem(me // pack + 1 + step, groups)
+        for b in range(pack):
+            block = g * pack + b
+
+            @pl.when(block != me)
+            def _():
+                p_copy(block, block).wait_recv()
+                q_copy(block, block).wait_recv()
+
+            named, rank = keys_of(pt_all[block], hot_count + me * list_dev, list_dev)
+            key[:, b * qcount : (b + 1) * qcount] = jnp.where(named, rank + float(cap * b), -1.0)
+        stack = q_all[pl.ds(g * pack, pack)].reshape(pack * qcount, q_ref.shape[1])
+        for l in range(list_dev):
+            rows_l = jnp.dot(match(l), stack, preferred_element_type=f32).astype(jnp.bfloat16)
+            work[pl.ds(l, lsize, stride=SUB), :] = lax.dot_general(
+                cold_ref[l], rows_l, (((1,), (1,)), ((), ())), preferred_element_type=f32
+            )
+        shorten()
+        for l in range(list_dev):
+            spread(l, half)
+        best_of(runs.at[0], 0, runs.at[1], 0, tmp, runs.at[0])
+        best_of(runs.at[2], 0, runs.at[3], 0, tmp, runs.at[2])
+        best_of(runs.at[0], 0, runs.at[2], 0, tmp, runs.at[0])
+        best_of(runs.at[0], 0, runs.at[0], 0, tmp, runs.at[1], turn=pack)
+        for b in range(pack):
+            block = g * pack + b
+            sendbuf[block] = runs[1, pl.ds(b, TOPK, stride=SUB), :]
+
+            @pl.when(block != me)
+            def _():
+                s_copy(block, me).start()
+
+    recv[me] = sendbuf[me]
+
+    @pl.loop(1, rows)
+    def _(d):
+        b = lax.rem(me + d, rows)
+        s_copy(b, b).wait_recv()
+
+    for o in range(rows):
+        runs[o // SUB, pl.ds(o % SUB, TOPK, stride=SUB), :] = recv[o]
+    for k in range(rows // SUB):
+        best_of(hotbest, 0, runs.at[k], 0, tmp, hotbest)
+    turn = SUB // 2
+    src, dst = hotbest, runs.at[0]
+    while turn:
+        best_of(src, 0, src, 0, tmp, dst, turn=turn)
+        src, dst = dst, src
+        turn //= 2
+    result = src[pl.ds(0, TOPK, stride=SUB), :]
+    out_ref[...] = result.T
+
+    @pl.loop(1, rows)
+    def _(d):
+        b = lax.rem(me + d, rows)
+        p_copy(b, me).wait_send()
+        q_copy(b, me).wait_send()
+        s_copy(b, me).wait_send()
+
+
+def shards(queries, probes, hot_lists, cold_lists):
+    rows = lax.axis_size("row")
+    qcount, nprobe = probes.shape
+    list_dev = cold_lists.shape[0]
+    hot_count, lsize, width = hot_lists.shape
+    cap = 2 * ((qcount * nprobe + list_dev * rows - 1) // (list_dev * rows))
+    pack = LANES // cap
+    fits = (
+        qcount == LANES and lsize == 2 * TOPK and list_dev == SUB and pack == 4
+        and hot_count == pack * pack and rows == 2 * SUB
+    )
+    if not fits:
+        return general(queries, probes, hot_lists, cold_lists)
+    vmem = pl.BlockSpec(memory_space=pltpu.VMEM)
+    dma = pltpu.SemaphoreType.DMA((rows,))
+    return pl.pallas_call(
+        functools.partial(fused, rows, cap),
+        out_shape=jax.ShapeDtypeStruct((qcount, TOPK), jnp.float32),
+        in_specs=[vmem] * 4,
+        out_specs=vmem,
+        scratch_shapes=[
+            pltpu.VMEM((rows, qcount, width), jnp.bfloat16),
+            pltpu.VMEM((rows, nprobe, qcount), jnp.int32),
+            pltpu.VMEM((list_dev, pack * qcount), jnp.float32),
+            pltpu.VMEM((list_dev, LANES, pack * qcount), jnp.bfloat16),
+            pltpu.VMEM((lsize * SUB, LANES), jnp.float32),
+            pltpu.VMEM((TOPK * SUB, LANES), jnp.float32),
+            pltpu.VMEM((TOPK * SUB, LANES), jnp.float32),
+            pltpu.VMEM((list_dev * pack // SUB, TOPK * SUB, LANES), jnp.float32),
+            pltpu.VMEM((TOPK * SUB, LANES), jnp.float32),
+            pltpu.VMEM((rows, TOPK, qcount), jnp.float32),
+            pltpu.VMEM((rows, TOPK, qcount), jnp.float32),
+            dma, dma, dma, dma, dma, dma,
+        ],
+        compiler_params=pltpu.CompilerParams(
+            collective_id=0, has_side_effects=True, vmem_limit_bytes=48 * 1024 * 1024
+        ),
+    )(queries, probes.T, hot_lists, cold_lists)
+
+
 def solution(mesh):
     placed = (
         P(("tenant", "row"), None),

time: 353 us -> 75 us (0.21)
  the two profiles are of different devices: /device:TPU:13 before, /device:TPU:11 now
where the time goes in v1:
time: 75 us; the launch traced here: 74.8 us
  Pallas kernels  69.8 us (93%)
  local copies, waits for them, and re-layouts  4.98 us (7%)
    pallas_call x1, Pallas kernels, shards(): pl.pallas_call(functools.partial(fused, rows, cap), out_shape=jax.ShapeDt...  69.8 us
    unnamed x9, local copies, waits for them, and re-layouts  4.98 us

profile of v1, /device:TPU:11, one launch (start us, length us, event | category | flops | bytes accessed | tf_op | source)
XLA Modules:
  0.0 74.8 jit_solution(18151486338140681163)
XLA Ops:
  0.0 0.0 copy-start
  0.0 1.6 %copy-done = bf16[16,256,256]{2,1,0:T(8,128)(2,1)S(1)} copy-done((bf16[16,256,256]{2,1,0:T(8,128)(2,1)S(1)}, bf16[16,256,256]{2,1,0:T(8,128)(2,1)}, u32[]{:S(2)}) %copy-start) | copy-done | bytes 2097176
  1.6 0.0 copy-start.1
  1.6 1.2 %copy-done.1 = bf16[8,256,256]{2,1,0:T(8,128)(2,1)S(1)} copy-done((bf16[8,256,256]{2,1,0:T(8,128)(2,1)S(1)}, bf16[8,256,256]{2,1,0:T(8,128)(2,1)}, u32[]{:S(2)}) %copy-start.1) | copy-done | bytes 1048600
  2.8 0.0 copy-start.2
  2.8 0.8 %copy-done.2 = bf16[128,256]{1,0:T(8,128)(2,1)S(1)} copy-done((bf16[128,256]{1,0:T(8,128)(2,1)S(1)}, bf16[128,256]{1,0:T(8,128)(2,1)}, u32[]{:S(2)}) %copy-start.2) | copy-done | bytes 65560
  3.7 0.0 copy-start.3
  3.7 0.7 copy-done.3
  4.4 69.8 %shard_map.46 = f32[128,128]{1,0:T(8,128)S(1)} custom-call(bf16[128,256]{1,0:T(8,128)(2,1)S(1)} %copy-done.2, s32[16,128]{1,0:T(8,128)S(1)} %bitcast.1, bf16[16,256,256]{2,1,0:T(8,128)(2,1)S(1)} %copy-done, bf16[8,256,256]{2,1,0:T(8,128)(2,1)S(1)} %copy-done.1), custom_call_target="tpu_custom_call" | custom-call | tf_op jit(solution)/shard_map/pallas_call | solution.py:393
  74.2 0.6 copy.6
Async XLA Ops:
  0.0 1.6 %copy-start = (bf16[16,256,256]{2,1,0:T(8,128)(2,1)S(1)}, bf16[16,256,256]{2,1,0:T(8,128)(2,1)}, u32[]{:S(2)}) copy-start(bf16[16,256,256]{2,1,0:T(8,128)(2,1)} %hot_ref.1) | copy-start | bytes 6291460
  1.6 1.2 %copy-start.1 = (bf16[8,256,256]{2,1,0:T(8,128)(2,1)S(1)}, bf16[8,256,256]{2,1,0:T(8,128)(2,1)}, u32[]{:S(2)}) copy-start(bf16[8,256,256]{2,1,0:T(8,128)(2,1)} %cold_ref.1) | copy-start | bytes 3145732
  2.8 0.8 %copy-start.2 = (bf16[128,256]{1,0:T(8,128)(2,1)S(1)}, bf16[128,256]{1,0:T(8,128)(2,1)}, u32[]{:S(2)}) copy-start(bf16[128,256]{1,0:T(8,128)(2,1)} %q_ref.1) | copy-start | bytes 196612
  3.7 0.7 copy-start.3

commit v2 on v1

--- a/solution.py
+++ b/solution.py
@@ -192,37 +192,60 @@
 
 
 def fused(
-    rows, cap, q_ref, pt_ref, hot_ref, cold_ref, out_ref,
-    q_all, pt_all, key, onehot, work, short, tmp, runs, hotbest, sendbuf, recv,
-    qs_sem, qr_sem, ps_sem, pr_sem, ss_sem, sr_sem,
+    rows, cap, q_ref, hot_ref, cold_ref, out_ref,
+    q_all, key, onehot, work, short, tmp, runs, hotbest, keep, pairbuf, sendbuf, mergebuf, recv,
+    gs_sem, gr_sem, ps_sem, pr_sem, ss_sem, sr_sem,
 ):
     me = lax.axis_index("row")
-    qcount = q_ref.shape[0]
+    core = lax.rem(me, 2)
+    partner = me + 1 - 2 * core
+    across = me + 2 - 4 * lax.rem(me // 2, 2)
     hot_count, lsize = hot_ref.shape[0], hot_ref.shape[1]
+    qcount = LANES
+    nprobe = q_ref.shape[0] - qcount
     list_dev = cold_ref.shape[0]
-    nprobe = pt_ref.shape[0]
     pack = LANES // cap
+    groups = rows // pack
     f32 = jnp.float32
 
-    def peer(b):
-        return {"row": b}
-
-    def q_copy(b, slot):
+    def remote(src, dst, send_sem, recv_sem, to):
         return pltpu.make_async_remote_copy(
-            src_ref=q_ref, dst_ref=q_all.at[slot], send_sem=qs_sem.at[b], recv_sem=qr_sem.at[slot],
-            device_id=peer(b), device_id_type=pl.DeviceIdType.MESH,
+            src_ref=src, dst_ref=dst, send_sem=send_sem, recv_sem=recv_sem,
+            device_id={"row": to}, device_id_type=pl.DeviceIdType.MESH,
         )
 
-    def p_copy(b, slot):
-        return pltpu.make_async_remote_copy(
-            src_ref=pt_ref, dst_ref=pt_all.at[slot], send_sem=ps_sem.at[b], recv_sem=pr_sem.at[slot],
-            device_id=peer(b), device_id_type=pl.DeviceIdType.MESH,
+    def gather_copy(source, kind, step, to):
+        src = q_ref if step == 0 and kind != 2 else q_all.at[source]
+        return remote(src, q_all.at[source], gs_sem.at[kind, step], gr_sem.at[source], to)
+
+    def line(step):
+        return lax.rem(me + pack * step, rows)
+
+    def column(step):
+        return lax.rem(across + pack * step, rows)
+
+    def arrived(source):
+        gather_copy(source, 2, 0, partner).wait_recv()
+
+    def relay_line(step):
+        if step:
+            arrived(line(step))
+        gather_copy(line(step), 0, step, across).start()
+        gather_copy(line(step), 1, step, partner).start()
+
+    def relay_column(step):
+        arrived(column(step))
+        gather_copy(column(step), 2, step, partner).start()
+
+    def pair_copy(step, k):
+        return remote(
+            sendbuf.at[step, 2 * k + 1 - core], pairbuf.at[step, k],
+            ps_sem.at[step, k], pr_sem.at[step, k], partner,
         )
 
-    def s_copy(b, slot):
-        return pltpu.make_async_remote_copy(
-            src_ref=sendbuf.at[b], dst_ref=recv.at[slot], send_sem=ss_sem.at[b],
-            recv_sem=sr_sem.at[slot], device_id=peer(b), device_id_type=pl.DeviceIdType.MESH,
+    def final_copy(step, k, to, source):
+        return remote(
+            mergebuf.at[step, 2 * k + core], recv.at[source], ss_sem.at[step, k], sr_sem.at[source], to
         )
 
     barrier = pltpu.get_barrier_semaphore()
@@ -230,19 +253,18 @@
     @pl.loop(1, rows)
     def _(d):
         pl.semaphore_signal(
-            barrier, inc=1, device_id=peer(lax.rem(me + d, rows)), device_id_type=pl.DeviceIdType.MESH
+            barrier, inc=1, device_id={"row": lax.rem(me + d, rows)},
+            device_id_type=pl.DeviceIdType.MESH,
         )
 
     pl.semaphore_wait(barrier, rows - 1)
 
-    @pl.loop(1, rows)
-    def _(d):
-        b = lax.rem(me + d, rows)
-        p_copy(b, me).start()
-        q_copy(b, me).start()
-
+    relay_line(0)
+    for step in range(1, groups):
+        remote(
+            q_ref, q_all.at[me], gs_sem.at[3, step], gr_sem.at[me], lax.rem(me + rows - pack * step, rows)
+        ).start()
     q_all[me] = q_ref[...]
-    pt_all[me] = pt_ref[...]
 
     before = (
         lax.broadcasted_iota(jnp.int32, (qcount, qcount), 0)
@@ -251,7 +273,8 @@
     before = jnp.where(before, 1.0, 0.0).astype(jnp.bfloat16)
 
     def keys_of(pt, first, count):
-        ids = first + lax.broadcasted_iota(jnp.int32, (count, qcount), 0)
+        ids = (first + lax.broadcasted_iota(jnp.int32, (count, qcount), 0)).astype(f32)
+        pt = pt.astype(f32)
         named = pt[0:1, :] == ids
         for j in range(1, nprobe):
             named = named | (pt[j : j + 1, :] == ids)
@@ -289,11 +312,11 @@
 
     half = SUB // pack
 
-    named, rank = keys_of(pt_ref[...], 0, hot_count)
+    named, rank = keys_of(q_ref[qcount : qcount + nprobe, :qcount], 0, hot_count)
     for l in range(hot_count):
         value = jnp.where(named[l : l + 1, :], rank[l : l + 1, :] + float(cap * (l % pack)), -1.0)
         key[l // pack : l // pack + 1, (l % pack) * qcount : (l % pack + 1) * qcount] = value
-    mine = q_ref[...]
+    mine = q_ref[:qcount, :]
     stack = jnp.concatenate([mine] * pack, axis=0)
     for t in range(hot_count // pack):
         rows_t = jnp.dot(match(t), stack, preferred_element_type=f32).astype(jnp.bfloat16)
@@ -304,60 +327,91 @@
             )
             score = one if score is None else jnp.where(lane >= c * cap, one, score)
         work[pl.ds(t, lsize, stride=SUB), :] = score
-        if hot_count // pack + t < SUB:
-            work[pl.ds(hot_count // pack + t, lsize, stride=SUB), :] = score
+        work[pl.ds(hot_count // pack + t, lsize, stride=SUB), :] = score
+    relay_column(0)
     shorten()
+    relay_line(1)
     for t in range(hot_count // pack):
         spread(t, half)
     best_of(runs.at[0], 0, runs.at[1], 0, tmp, hotbest)
-
-    groups = rows // pack
+    relay_line(2)
+    relay_column(1)
+
+    def merge_out(step):
+        g = lax.rem(me // pack + step, groups)
+        for k in range(pack // 2):
+            pair_copy(step, k).wait_recv()
+            part = pairbuf[step, k]
+            for c in range(2):
+                runs[3, pl.ds(2 * k + c, TOPK, stride=SUB), :] = part
+        best_of(keep.at[step], 0, runs.at[3], 0, tmp, runs.at[2])
+        for b in range(pack):
+            mergebuf[step, b] = runs[2, pl.ds(b, TOPK, stride=SUB), :]
+        for k in range(pack // 2):
+            to = g * pack + 2 * k + core
+
+            @pl.when(to != me)
+            def _():
+                final_copy(step, k, to, me // 2).start()
+
+            @pl.when(to == me)
+            def _():
+                recv[me // 2] = mergebuf[step, 2 * k + core]
 
     @pl.loop(0, groups)
     def _(step):
-        g = lax.rem(me // pack + 1 + step, groups)
+        g = lax.rem(me // pack + step, groups)
+        arrived(lax.rem(partner + pack * step, rows))
+        arrived(lax.rem(across + partner - me + pack * step, rows))
         for b in range(pack):
             block = g * pack + b
-
-            @pl.when(block != me)
-            def _():
-                p_copy(block, block).wait_recv()
-                q_copy(block, block).wait_recv()
-
-            named, rank = keys_of(pt_all[block], hot_count + me * list_dev, list_dev)
+            named, rank = keys_of(
+                q_all[block, qcount : qcount + nprobe, :qcount], hot_count + me * list_dev, list_dev
+            )
             key[:, b * qcount : (b + 1) * qcount] = jnp.where(named, rank + float(cap * b), -1.0)
-        stack = q_all[pl.ds(g * pack, pack)].reshape(pack * qcount, q_ref.shape[1])
+        stack = jnp.concatenate([q_all[g * pack + b, :qcount, :] for b in range(pack)], axis=0)
         for l in range(list_dev):
             rows_l = jnp.dot(match(l), stack, preferred_element_type=f32).astype(jnp.bfloat16)
             work[pl.ds(l, lsize, stride=SUB), :] = lax.dot_general(
                 cold_ref[l], rows_l, (((1,), (1,)), ((), ())), preferred_element_type=f32
             )
+
+        @pl.when(step == 0)
+        def _():
+            relay_line(3)
+            relay_column(2)
+
         shorten()
+
+        @pl.when(step == 0)
+        def _():
+            relay_column(3)
+
+        @pl.when(step >= 1)
+        def _():
+            merge_out(step - 1)
+
         for l in range(list_dev):
             spread(l, half)
         best_of(runs.at[0], 0, runs.at[1], 0, tmp, runs.at[0])
         best_of(runs.at[2], 0, runs.at[3], 0, tmp, runs.at[2])
         best_of(runs.at[0], 0, runs.at[2], 0, tmp, runs.at[0])
-        best_of(runs.at[0], 0, runs.at[0], 0, tmp, runs.at[1], turn=pack)
+        best_of(runs.at[0], 0, runs.at[0], 0, tmp, keep.at[step], turn=pack)
         for b in range(pack):
-            block = g * pack + b
-            sendbuf[block] = runs[1, pl.ds(b, TOPK, stride=SUB), :]
-
-            @pl.when(block != me)
-            def _():
-                s_copy(block, me).start()
-
-    recv[me] = sendbuf[me]
-
-    @pl.loop(1, rows)
+            sendbuf[step, b] = keep[step, pl.ds(b, TOPK, stride=SUB), :]
+        for k in range(pack // 2):
+            pair_copy(step, k).start()
+
+    merge_out(groups - 1)
+
+    @pl.loop(1, rows // 2)
     def _(d):
-        b = lax.rem(me + d, rows)
-        s_copy(b, b).wait_recv()
-
-    for o in range(rows):
-        runs[o // SUB, pl.ds(o % SUB, TOPK, stride=SUB), :] = recv[o]
-    for k in range(rows // SUB):
-        best_of(hotbest, 0, runs.at[k], 0, tmp, hotbest)
+        source = lax.rem(me // 2 + d, rows // 2)
+        final_copy(0, 0, partner, source).wait_recv()
+
+    for o in range(rows // 2):
+        runs[0, pl.ds(o, TOPK, stride=SUB), :] = recv[o]
+    best_of(hotbest, 0, runs.at[0], 0, tmp, hotbest)
     turn = SUB // 2
     src, dst = hotbest, runs.at[0]
     while turn:
@@ -367,12 +421,19 @@
     result = src[pl.ds(0, TOPK, stride=SUB), :]
     out_ref[...] = result.T
 
-    @pl.loop(1, rows)
-    def _(d):
-        b = lax.rem(me + d, rows)
-        p_copy(b, me).wait_send()
-        q_copy(b, me).wait_send()
-        s_copy(b, me).wait_send()
+    for step in range(groups):
+        gather_copy(line(step), 0, step, across).wait_send()
+        gather_copy(line(step), 1, step, partner).wait_send()
+        gather_copy(column(step), 2, step, partner).wait_send()
+        if step:
+            remote(q_ref, q_all.at[me], gs_sem.at[3, step], gr_sem.at[me], partner).wait_send()
+        for k in range(pack // 2):
+            pair_copy(step, k).wait_send()
+            to = lax.rem(me // pack + step, groups) * pack + 2 * k + core
+
+            @pl.when(to != me)
+            def _():
+                final_copy(step, k, to, me // 2).wait_send()
 
 
 def shards(queries, probes, hot_lists, cold_lists):
@@ -384,35 +445,47 @@
     pack = LANES // cap
     fits = (
         qcount == LANES and lsize == 2 * TOPK and list_dev == SUB and pack == 4
-        and hot_count == pack * pack and rows == 2 * SUB
+        and hot_count == pack * pack and rows == 2 * SUB and width >= qcount
+        and hot_count + list_dev * rows <= 256
     )
     if not fits:
         return general(queries, probes, hot_lists, cold_lists)
     vmem = pl.BlockSpec(memory_space=pltpu.VMEM)
-    dma = pltpu.SemaphoreType.DMA((rows,))
+    dma = pltpu.SemaphoreType.DMA
+    groups = rows // pack
+    ids = jnp.pad(probes.T, ((0, 0), (0, width - qcount))).astype(jnp.bfloat16)
+    held = jnp.concatenate([queries, ids], axis=0)
+    run = pltpu.VMEM((TOPK * SUB, LANES), jnp.float32)
     return pl.pallas_call(
         functools.partial(fused, rows, cap),
         out_shape=jax.ShapeDtypeStruct((qcount, TOPK), jnp.float32),
-        in_specs=[vmem] * 4,
+        in_specs=[vmem] * 3,
         out_specs=vmem,
         scratch_shapes=[
-            pltpu.VMEM((rows, qcount, width), jnp.bfloat16),
-            pltpu.VMEM((rows, nprobe, qcount), jnp.int32),
+            pltpu.VMEM((rows,) + held.shape, jnp.bfloat16),
             pltpu.VMEM((list_dev, pack * qcount), jnp.float32),
             pltpu.VMEM((list_dev, LANES, pack * qcount), jnp.bfloat16),
             pltpu.VMEM((lsize * SUB, LANES), jnp.float32),
-            pltpu.VMEM((TOPK * SUB, LANES), jnp.float32),
-            pltpu.VMEM((TOPK * SUB, LANES), jnp.float32),
+            run,
+            run,
             pltpu.VMEM((list_dev * pack // SUB, TOPK * SUB, LANES), jnp.float32),
-            pltpu.VMEM((TOPK * SUB, LANES), jnp.float32),
-            pltpu.VMEM((rows, TOPK, qcount), jnp.float32),
-            pltpu.VMEM((rows, TOPK, qcount), jnp.float32),
-            dma, dma, dma, dma, dma, dma,
+            run,
+            pltpu.VMEM((groups, TOPK * SUB, LANES), jnp.float32),
+            pltpu.VMEM((groups, pack // 2, TOPK, qcount), jnp.float32),
+            pltpu.VMEM((groups, pack, TOPK, qcount), jnp.float32),
+            pltpu.VMEM((groups, pack, TOPK, qcount), jnp.float32),
+            pltpu.VMEM((rows // 2, TOPK, qcount), jnp.float32),
+            dma((4, groups)),
+            dma((rows,)),
+            dma((groups, pack // 2)),
+            dma((groups, pack // 2)),
+            dma((groups, pack // 2)),
+            dma((rows // 2,)),
         ],
         compiler_params=pltpu.CompilerParams(
             collective_id=0, has_side_effects=True, vmem_limit_bytes=48 * 1024 * 1024
         ),
-    )(queries, probes.T, hot_lists, cold_lists)
+    )(held, hot_lists, cold_lists)
 
 
 def solution(mesh):

time: 75 us -> 49.7 us (0.66)
  the two profiles are of different devices: /device:TPU:11 before, /device:TPU:0 now
where the time goes in v2:
time: 49.7 us; the launch traced here: 49.5 us
  Pallas kernels  44.5 us (90%)
  local copies, waits for them, and re-layouts  3.45 us (7%)
  other arithmetic  1.54 us (3%)
    pallas_call x1, Pallas kernels, shards(): pl.pallas_call(functools.partial(fused, rows, cap), out_shape=jax.ShapeDt...  44.5 us
    unnamed x5, local copies, waits for them, and re-layouts  3.45 us

profile of v2, /device:TPU:0, one launch (start us, length us, event | category | flops | bytes accessed | tf_op | source)
XLA Modules:
  0.0 49.5 jit_solution(10748291530309810461)
XLA Ops:
  0.0 0.7 %convert_bitcast_fusion = bf16[16,128]{1,0:T(8,128)(2,1)S(1)} fusion(s32[128,16]{0,1:T(8,128)} %param.5), kind=kLoop, calls=%fused_computation.3 | loop fusion | flops 2048 | bytes 12288 | tf_op jit(solution)/shard_map/transpose | solution.py:456
  0.7 0.8 %fusion.1.q_ref = bf16[144,256]{1,0:T(8,128)(2,1)S(1)} fusion(bf16[16,128]{1,0:T(8,128)(2,1)S(1)} %convert_bitcast_fusion, bf16[128,256]{1,0:T(8,128)(2,1)} %param.4), kind=kLoop, calls=%fused_computation.2 | loop fusion | flops 221184 | bytes 143360 | tf_op jit(solution)/shard_map/concatenate | solution.py:457
  1.5 0.0 copy-start
  1.5 1.6 %copy-done = bf16[16,256,256]{2,1,0:T(8,128)(2,1)S(1)} copy-done((bf16[16,256,256]{2,1,0:T(8,128)(2,1)S(1)}, bf16[16,256,256]{2,1,0:T(8,128)(2,1)}, u32[]{:S(2)}) %copy-start) | copy-done | bytes 2097176
  3.1 0.0 copy-start.1
  3.1 1.2 %copy-done.1 = bf16[8,256,256]{2,1,0:T(8,128)(2,1)S(1)} copy-done((bf16[8,256,256]{2,1,0:T(8,128)(2,1)S(1)}, bf16[8,256,256]{2,1,0:T(8,128)(2,1)}, u32[]{:S(2)}) %copy-start.1) | copy-done | bytes 1048600
  4.4 44.5 %shard_map.46 = f32[128,128]{1,0:T(8,128)S(1)} custom-call(bf16[144,256]{1,0:T(8,128)(2,1)S(1)} %fusion.1.q_ref, bf16[16,256,256]{2,1,0:T(8,128)(2,1)S(1)} %copy-done, bf16[8,256,256]{2,1,0:T(8,128)(2,1)S(1)} %copy-done.1), custom_call_target="tpu_custom_call" | custom-call | tf_op jit(solution)/shard_map/pallas_call | solution.py:459
  48.8 0.6 %copy.6 = f32[128,128]{1,0:T(8,128)} copy(f32[128,128]{1,0:T(8,128)S(1)} %shard_map.46) | data formatting | bytes 131072
Async XLA Ops:
  1.5 1.6 %copy-start = (bf16[16,256,256]{2,1,0:T(8,128)(2,1)S(1)}, bf16[16,256,256]{2,1,0:T(8,128)(2,1)}, u32[]{:S(2)}) copy-start(bf16[16,256,256]{2,1,0:T(8,128)(2,1)} %hot_ref.1) | copy-start | bytes 6291460
  3.1 1.2 %copy-start.1 = (bf16[8,256,256]{2,1,0:T(8,128)(2,1)S(1)}, bf16[8,256,256]{2,1,0:T(8,128)(2,1)}, u32[]{:S(2)}) copy-start(bf16[8,256,256]{2,1,0:T(8,128)(2,1)} %cold_ref.1) | copy-start | bytes 3145732

commit v3 on v2

--- a/solution.py
+++ b/solution.py
@@ -99,53 +99,36 @@
 
 
 def at(i):
-    return pl.ds(pl.multiple_of(i * SUB, SUB), SUB)
-
-
-def loop(n, unroll, body):
-    @pl.loop(0, n // unroll)
-    def _(step):
-        for u in range(unroll):
-            body(step * unroll + u)
+    return pl.ds(i * SUB, SUB)
 
 
 def sort_runs(ref, count):
     net = batcher(32)
 
-    def body(t):
-        vals = [ref[at(t * 32 + i), :] for i in range(32)]
+    @pl.loop(0, count // 32)
+    def _(t):
+        start = pl.multiple_of(t * (32 * SUB), 32 * SUB)
+        vals = [ref[pl.ds(start + i * SUB, SUB), :] for i in range(32)]
         for a, b in net:
             exchange(vals, a, b)
         for i in range(32):
-            ref[at(t * 32 + i), :] = vals[i]
-
-    loop(count // 32, 1, body)
+            ref[pl.ds(start + i * SUB, SUB), :] = vals[i]
 
 
 def join_runs(ref, count, half):
     size = 2 * half
     step = half // 4
-    per = 4
-
-    @pl.loop(0, count // size * step // per)
-    def _(t):
-        base = t * per // step * size
-        first = t * per % step
-        work = []
-        for u in range(per):
-            i = first + u
-            idx = [base + i + step * k for k in range(4)]
-            idx += [base + size - 1 - i - step * k for k in range(4)]
-            work.append((idx, [ref[at(x), :] for x in idx]))
-        for _, vals in work:
+    for base in range(0, count, size):
+        for i in range(base, base + step):
+            idx = [i + step * k for k in range(4)]
+            idx += [2 * base + size - 1 - x for x in idx]
+            vals = [ref[at(x), :] for x in idx]
             for k in range(4):
                 exchange(vals, k, 4 + k)
             clean(vals, [0, 1, 2, 3], (2, 1))
             clean(vals, [7, 6, 5, 4], (2, 1))
-        for idx, vals in work:
             for x, v in zip(idx, vals):
                 ref[at(x), :] = v
-
     tidy(ref, ref, count, step)
 
 
@@ -155,47 +138,38 @@
     while d:
         dists.append(d)
         d //= 2
-
-    @pl.loop(0, count // 32)
-    def _(t):
-        vals = [src[at(t * 32 + i), :] for i in range(32)]
-        for c in range(32 // block):
-            clean(vals, list(range(c * block, (c + 1) * block)), dists)
-        for i in range(32):
-            dst[at(t * 32 + i), :] = vals[i]
+    for start in range(0, count, block):
+        vals = [src[at(start + i), :] for i in range(block)]
+        clean(vals, list(range(block)), dists)
+        for i in range(block):
+            dst[at(start + i), :] = vals[i]
 
 
 def best_of(a, abase, b, bbase, tmp, dst, turn=0):
     step = TOPK // 8
-    per = 2
-
-    @pl.loop(0, step // per)
-    def _(t):
-        work = []
-        for u in range(per):
-            i = t * per + u
-            vals = []
-            for k in range(8):
-                x = a[at(abase + i + step * k), :]
-                y = b[at(bbase + TOPK - 1 - i - step * k), :]
-                if turn:
-                    y = pltpu.roll(y, turn, 0)
-                vals.append(jnp.maximum(x, y))
-            work.append(vals)
-        for vals in work:
-            clean(vals, list(range(8)), (4, 2, 1))
-        for u, vals in enumerate(work):
-            for k in range(8):
-                tmp[at(t * per + u + step * k), :] = vals[k]
-
+    for i in range(step):
+        vals = []
+        for k in range(8):
+            x = a[at(abase + i + step * k), :]
+            y = b[at(bbase + TOPK - 1 - i - step * k), :]
+            if turn:
+                y = pltpu.roll(y, turn, 0)
+            vals.append(jnp.maximum(x, y))
+        clean(vals, list(range(8)), (4, 2, 1))
+        for k in range(8):
+            tmp[at(i + step * k), :] = vals[k]
     tidy(tmp, dst, TOPK, step)
 
 
 def fused(
-    rows, cap, q_ref, hot_ref, cold_ref, out_ref,
-    q_all, key, onehot, work, short, tmp, runs, hotbest, keep, pairbuf, sendbuf, mergebuf, recv,
+    rows, cap, q_ref, hot_hbm, cold_hbm, out_ref,
+    hot_ref, cold_ref, list_sem, q_all, key, onehot, work, short, tmp, runs, hotbest, keep, pairbuf, sendbuf, mergebuf, recv,
     gs_sem, gr_sem, ps_sem, pr_sem, ss_sem, sr_sem,
 ):
+    fetch_hot = pltpu.make_async_copy(hot_hbm, hot_ref, list_sem.at[0])
+    fetch_cold = pltpu.make_async_copy(cold_hbm, cold_ref, list_sem.at[1])
+    fetch_hot.start()
+    fetch_cold.start()
     me = lax.axis_index("row")
     core = lax.rem(me, 2)
     partner = me + 1 - 2 * core
@@ -318,6 +292,7 @@
         key[l // pack : l // pack + 1, (l % pack) * qcount : (l % pack + 1) * qcount] = value
     mine = q_ref[:qcount, :]
     stack = jnp.concatenate([mine] * pack, axis=0)
+    fetch_hot.wait()
     for t in range(hot_count // pack):
         rows_t = jnp.dot(match(t), stack, preferred_element_type=f32).astype(jnp.bfloat16)
         score = None
@@ -336,6 +311,7 @@
     best_of(runs.at[0], 0, runs.at[1], 0, tmp, hotbest)
     relay_line(2)
     relay_column(1)
+    fetch_cold.wait()
 
     def merge_out(step):
         g = lax.rem(me // pack + step, groups)
@@ -451,6 +427,7 @@
     if not fits:
         return general(queries, probes, hot_lists, cold_lists)
     vmem = pl.BlockSpec(memory_space=pltpu.VMEM)
+    far = pl.BlockSpec(memory_space=pl.ANY)
     dma = pltpu.SemaphoreType.DMA
     groups = rows // pack
     ids = jnp.pad(probes.T, ((0, 0), (0, width - qcount))).astype(jnp.bfloat16)
@@ -459,9 +436,12 @@
     return pl.pallas_call(
         functools.partial(fused, rows, cap),
         out_shape=jax.ShapeDtypeStruct((qcount, TOPK), jnp.float32),
-        in_specs=[vmem] * 3,
+        in_specs=[vmem, far, far],
         out_specs=vmem,
         scratch_shapes=[
+            pltpu.VMEM(hot_lists.shape, jnp.bfloat16),
+            pltpu.VMEM(cold_lists.shape, jnp.bfloat16),
+            dma((2,)),
             pltpu.VMEM((rows,) + held.shape, jnp.bfloat16),
             pltpu.VMEM((list_dev, pack * qcount), jnp.float32),
             pltpu.VMEM((list_dev, LANES, pack * qcount), jnp.bfloat16),
@@ -483,7 +463,7 @@
             dma((rows // 2,)),
         ],
         compiler_params=pltpu.CompilerParams(
-            collective_id=0, has_side_effects=True, vmem_limit_bytes=48 * 1024 * 1024
+            collective_id=0, has_side_effects=True, vmem_limit_bytes=60 * 1024 * 1024
         ),
     )(held, hot_lists, cold_lists)
 

time: 49.7 us -> 46.7 us (0.940)
  local copies, waits for them, and re-layouts: 3.45 us -> 1.47 us
  Pallas kernels: 44.5 us -> 42.8 us
  other arithmetic: 1.54 us -> 2.17 us
    unnamed x5 -> x1, local copies, waits for them, and re-layouts: 3.45 us -> 1.47 us
    pallas_call x1, Pallas kernels: 44.5 us -> 42.8 us  [shards(): pl.pallas_call(functools.partial(fused, rows, cap), out_shape=jax.ShapeDt...]
    concatenate x1, other arithmetic: 0.85 us -> 1.47 us  [shards(): held = jnp.concatenate([queries, ids], axis=0)]
where the time goes in v3:
time: 46.7 us; the launch traced here: 46.4 us
  Pallas kernels  42.8 us (92%)
  other arithmetic  2.17 us (5%)
  local copies, waits for them, and re-layouts  1.47 us (3%)
    pallas_call x1, Pallas kernels, shards(): pl.pallas_call(functools.partial(fused, rows, cap), out_shape=jax.ShapeDt...  42.8 us
    unnamed x1, local copies, waits for them, and re-layouts  1.47 us
    concatenate x1, other arithmetic, shards(): held = jnp.concatenate([queries, ids], axis=0)  1.47 us

profile of v3, /device:TPU:0, one launch (start us, length us, event | category | flops | bytes accessed | tf_op | source)
XLA Modules:
  0.0 46.4 jit_solution(13554506534478002197)
XLA Ops:
  0.0 0.7 %convert_bitcast_fusion = bf16[16,128]{1,0:T(8,128)(2,1)S(1)} fusion(s32[128,16]{0,1:T(8,128)} %param.5), kind=kLoop, calls=%fused_computation.3 | loop fusion | flops 2048 | bytes 12288 | tf_op jit(solution)/shard_map/transpose | solution.py:433
  0.7 1.5 %fusion.1.q_ref = bf16[144,256]{1,0:T(8,128)(2,1)} fusion(bf16[16,128]{1,0:T(8,128)(2,1)S(1)} %convert_bitcast_fusion, bf16[128,256]{1,0:T(8,128)(2,1)} %param.4), kind=kLoop, calls=%fused_computation.2 | loop fusion | flops 221184 | bytes 143360 | tf_op jit(solution)/shard_map/concatenate | solution.py:434
  2.2 42.8 %shard_map.46 = f32[128,128]{1,0:T(8,128)} custom-call(bf16[144,256]{1,0:T(8,128)(2,1)} %fusion.1.q_ref, bf16[16,256,256]{2,1,0:T(8,128)(2,1)} %hot_hbm.1, bf16[8,256,256]{2,1,0:T(8,128)(2,1)} %cold_hbm.1), custom_call_target="tpu_custom_call" | custom-call | tf_op jit(solution)/shard_map/pallas_call | solution.py:436
  44.9 1.5 %copy.6 = f32[128,128]{1,0:T(8,128)} copy(f32[128,128]{1,0:T(8,128)} %shard_map.46) | data formatting | bytes 131072

commit v4 on v3

--- a/solution.py
+++ b/solution.py
@@ -269,9 +269,9 @@
         part = short[pl.ds(l, TOPK, stride=SUB), :]
         high = part.astype(jnp.bfloat16)
         low = (part - high.astype(f32)).astype(jnp.bfloat16)
-        hot1 = onehot[l]
-        full = jnp.dot(high, hot1, preferred_element_type=f32)
-        full = full + jnp.dot(low, hot1, preferred_element_type=f32)
+        both = jnp.concatenate([high, low], axis=0)
+        full = jnp.dot(both, onehot[l], preferred_element_type=f32)
+        full = full[:TOPK, :] + full[TOPK:, :]
         full = jnp.where(key[l : l + 1, :] >= 0.0, full, LOW)
         for b in range(pack):
             runs[l // half, pl.ds((l % half) * pack + b, TOPK, stride=SUB), :] = full[
@@ -347,9 +347,14 @@
             key[:, b * qcount : (b + 1) * qcount] = jnp.where(named, rank + float(cap * b), -1.0)
         stack = jnp.concatenate([q_all[g * pack + b, :qcount, :] for b in range(pack)], axis=0)
         for l in range(list_dev):
-            rows_l = jnp.dot(match(l), stack, preferred_element_type=f32).astype(jnp.bfloat16)
+            match(l)
+        every = jnp.dot(
+            onehot[...].reshape(list_dev * LANES, pack * qcount), stack, preferred_element_type=f32
+        ).astype(jnp.bfloat16)
+        for l in range(list_dev):
             work[pl.ds(l, lsize, stride=SUB), :] = lax.dot_general(
-                cold_ref[l], rows_l, (((1,), (1,)), ((), ())), preferred_element_type=f32
+                cold_ref[l], every[l * LANES : (l + 1) * LANES, :], (((1,), (1,)), ((), ())),
+                preferred_element_type=f32,
             )
 
         @pl.when(step == 0)

time: 46.7 us -> 46.9 us (level)
  no operation moved by 1% of the time
where the time goes in v4:
time: 46.9 us; the launch traced here: 46.7 us
  Pallas kernels  43 us (92%)
  other arithmetic  2.17 us (5%)
  local copies, waits for them, and re-layouts  1.47 us (3%)
    pallas_call x1, Pallas kernels, shards(): pl.pallas_call(functools.partial(fused, rows, cap), out_shape=jax.ShapeDt...  43 us
    unnamed x1, local copies, waits for them, and re-layouts  1.47 us
    concatenate x1, other arithmetic, shards(): held = jnp.concatenate([queries, ids], axis=0)  1.47 us

profile of v4, /device:TPU:0, one launch (start us, length us, event | category | flops | bytes accessed | tf_op | source)
XLA Modules:
  0.0 46.7 jit_solution(17617215616251777086)
XLA Ops:
  0.0 0.7 %convert_bitcast_fusion = bf16[16,128]{1,0:T(8,128)(2,1)S(1)} fusion(s32[128,16]{0,1:T(8,128)} %param.5), kind=kLoop, calls=%fused_computation.3 | loop fusion | flops 2048 | bytes 12288 | tf_op jit(solution)/shard_map/transpose | solution.py:438
  0.7 1.5 %fusion.1.q_ref = bf16[144,256]{1,0:T(8,128)(2,1)} fusion(bf16[16,128]{1,0:T(8,128)(2,1)S(1)} %convert_bitcast_fusion, bf16[128,256]{1,0:T(8,128)(2,1)} %param.4), kind=kLoop, calls=%fused_computation.2 | loop fusion | flops 221184 | bytes 143360 | tf_op jit(solution)/shard_map/concatenate | solution.py:439
  2.2 43.0 %shard_map.46 = f32[128,128]{1,0:T(8,128)} custom-call(bf16[144,256]{1,0:T(8,128)(2,1)} %fusion.1.q_ref, bf16[16,256,256]{2,1,0:T(8,128)(2,1)} %hot_hbm.1, bf16[8,256,256]{2,1,0:T(8,128)(2,1)} %cold_hbm.1), custom_call_target="tpu_custom_call" | custom-call | tf_op jit(solution)/shard_map/pallas_call | solution.py:441
  45.2 1.5 %copy.6 = f32[128,128]{1,0:T(8,128)} copy(f32[128,128]{1,0:T(8,128)} %shard_map.46) | data formatting | bytes 131072
